TPU v7x, 32 devices: a whole 2x2x4 slice. The times are simulated.
32 devices in a mesh: sub: 8 (over y, x, core), grp: 4 (over z).
Axes of the slice: x: 2, y: 2, z: 4, core: 2. Of those that a mesh axis runs over, the one named last changes fastest.
Arguments:
- res_inner: bfloat16 [2048, 16, 144], P(('sub', 'grp')), may hold values from -6 to 6
- res_face: bfloat16 [1024, 16, 144], P(('sub', 'grp')), may hold values from -6 to 6
- inner_inv: bfloat16 [2048, 144, 144], P(('sub', 'grp')), may hold values from -0.5 to 0.5
- face_coupling: bfloat16 [1024, 144, 144], P(('sub', 'grp')), may hold values from -0.5 to 0.5
- face_elem: int32 [32, 32], P(('sub', 'grp')), may hold values from 0 to 63
- face_inv: bfloat16 [1024, 144, 144], P(('sub', 'grp')), may hold values from -0.5 to 0.5
- coarse_basis: bfloat16 [1024, 64, 144], P(('sub', 'grp')), may hold values from -0.0625 to 0.0625
- coarse_map: int32 [32, 64], P(('sub', 'grp')), may hold values from 0 to 511
- coarse_inv: float32 [512, 512], P('grp'), as said below
- recv_index: int32 [32, 32], P(('sub', 'grp')), may hold values from 0 to 8, as said below
- sharers: int32 [32, 32], P(('sub', 'grp')), may hold values from 0 to 32, as said below
Outputs:
- inner_out: bfloat16 [2048, 16, 144], P(('sub', 'grp'))
- face_out: bfloat16 [1024, 16, 144], P(('sub', 'grp'))
Inputs may be any that keep to these rules, and one draw needn't show every extreme that they name: `recv_index`: row o gives, for each subdomain s at position s, the index among the 8 blocks owned by subdomain o that slot o of subdomain s refers to, or 8 where that slot is unused. `sharers`: for a used slot, the number of used slots of all subdomains that refer to the same owned block, up to all 32 of them, which some block reaches; 0 exactly for unused slots. coarse_inv is symmetric.
All inputs are finite; a program needn't handle non-finite values.
Results may differ from a plain program's by a relative error of at most 0.006.
Values may be sent and summed in bfloat16 or wider, within the bound.
No kernel may reach another device: no remote copies, remote signals or barrier semaphores. Data moves between devices by JAX's collectives and lax.ppermute only.
A program may use at most 128 MiB of HBM per device.

v0:
```python
import jax
import jax.numpy as jnp
from jax import lax
from jax.sharding import PartitionSpec as P


def send_out(partials):
    return lax.all_to_all(partials, ("sub", "grp"), split_axis=0, concat_axis=0, tiled=True)


def send_back(spread):
    return lax.all_to_all(spread, ("sub", "grp"), split_axis=0, concat_axis=0, tiled=True)


def body(
    res_inner,
    res_face,
    inner_inv,
    face_coupling,
    face_elem,
    face_inv,
    coarse_basis,
    coarse_map,
    coarse_inv,
    recv_index,
    sharers,
):
    num_faces = res_face.shape[0]
    num_owned = num_faces // 4
    elements = res_inner.shape[0]
    num_coarse = coarse_inv.shape[1]
    counts = sharers[0]
    weights = jnp.where(counts > 0, 1.0 / jnp.maximum(counts, 1).astype(jnp.float32), 0.0)
    owner_onehot = (
        recv_index[0][None, :] == jnp.arange(num_owned, dtype=jnp.int32)[:, None]
    ).astype(jnp.bfloat16)

    def assemble(partials):
        received = send_out(partials)
        flattened = received.reshape(num_faces, -1)
        owner_sum = jnp.dot(owner_onehot, flattened, preferred_element_type=jnp.float32).astype(
            jnp.bfloat16
        )
        spread = jnp.einsum(
            "of,ok->fk", owner_onehot, owner_sum, preferred_element_type=jnp.float32
        ).astype(jnp.bfloat16)
        return send_back(spread.reshape(partials.shape))

    inner_w = jnp.einsum(
        "erb,ecb->erc", res_inner, inner_inv, preferred_element_type=jnp.float32
    ).astype(jnp.bfloat16)
    nearby = inner_w[face_elem[0]]
    condensed = res_face.astype(jnp.float32) - jnp.einsum(
        "lrb,lcb->lrc", nearby, face_coupling, preferred_element_type=jnp.float32
    )
    sent = (weights[:, None, None] * condensed).astype(jnp.bfloat16)
    gathered = assemble(sent)
    restricted = (weights[:, None, None] * gathered.astype(jnp.float32)).astype(jnp.bfloat16)
    local_coarse = jnp.einsum(
        "ljb,lrb->jr", coarse_basis, restricted, preferred_element_type=jnp.float32
    )
    coarse_onehot = (
        coarse_map[0][None, :] == jnp.arange(num_coarse, dtype=jnp.int32)[:, None]
    ).astype(jnp.float32)
    partial_rhs = jnp.dot(coarse_onehot, local_coarse, precision=lax.Precision.HIGHEST)
    coarse_rhs = lax.psum(partial_rhs, ("sub", "grp"))
    row_part = jnp.dot(coarse_inv, coarse_rhs, precision=lax.Precision.HIGHEST)
    coarse_sol = lax.all_gather(row_part, "grp", axis=0, tiled=True)
    picked = jnp.einsum(
        "kj,kr->jr", coarse_onehot, coarse_sol, precision=lax.Precision.HIGHEST
    ).astype(jnp.bfloat16)
    coarse_part = jnp.einsum(
        "ljb,jr->lrb", coarse_basis, picked, preferred_element_type=jnp.float32
    )
    local_part = jnp.einsum(
        "lrb,lcb->lrc", restricted, face_inv, preferred_element_type=jnp.float32
    )
    weighted = (weights[:, None, None] * (coarse_part + local_part)).astype(jnp.bfloat16)
    face_out = assemble(weighted)
    contrib = jnp.einsum(
        "lrc,lcb->lrb", face_out, face_coupling, preferred_element_type=jnp.float32
    )
    elem_onehot = (face_elem[0][None, :] == jnp.arange(elements, dtype=jnp.int32)[:, None]).astype(
        jnp.float32
    )
    scattered = jnp.dot(
        elem_onehot, contrib.reshape(num_faces, -1), precision=lax.Precision.HIGHEST
    ).reshape(res_inner.shape)
    inner_rhs = (res_inner.astype(jnp.float32) - scattered).astype(jnp.bfloat16)
    inner_out = jnp.einsum(
        "erb,ecb->erc", inner_rhs, inner_inv, preferred_element_type=jnp.float32
    ).astype(jnp.bfloat16)
    return (inner_out, face_out)


def solution(mesh):
    return jax.shard_map(
        body,
        mesh=mesh,
        in_specs=(
            P(("sub", "grp"), None, None),
            P(("sub", "grp"), None, None),
            P(("sub", "grp"), None, None),
            P(("sub", "grp"), None, None),
            P(("sub", "grp"), None),
            P(("sub", "grp"), None, None),
            P(("sub", "grp"), None, None),
            P(("sub", "grp"), None),
            P("grp", None),
            P(("sub", "grp"), None),
            P(("sub", "grp"), None),
        ),
        out_specs=(P(("sub", "grp"), None, None), P(("sub", "grp"), None, None)),
        check_vma=False,
    )
```

profile of v0, /device:TPU:0, one launch (start us, length us, event | category | flops | bytes accessed | tf_op | source)
XLA Modules:
  0.0 140.8 jit_solution(13594599169915256372)
XLA Ops:
  0.6 0.8 fusion.20
  1.5 0.7 fusion.19
  2.1 3.8 %convolution_convert_fusion.5 = bf16[64,16,144]{2,1,0:T(8,128)(2,1)S(1)} fusion(bf16[64,16,144]{2,1,0:T(8,128)(2,1)} %param.11, bf16[64,144,144]{2,1,0:T(8,128)(2,1)} %param.13), kind=kOutput, calls=%fused_computation.6 | convolution fusion | flops 42614784 | bytes 3244032 | tf_op jit(solution)/shard_map/erb,ecb->erc/dot_general | solution.py:49
  6.0 1.3 gather_fusion
  7.3 1.8 %fusion.2 = bf16[32,16,144]{2,1,0:T(8,128)(2,1)S(1)} fusion(bf16[32,16,144]{2,1,0:T(8,128)(2,1)} %gather_fusion, bf16[32,144,144]{2,1,0:T(8,128)(2,1)S(1)} %copy-done, bf16[32,16,144]{2,1,0:T(8,128)(2,1)} %param.12, f32[32]{0:T(128)S(1)} %fusion.20), kind=kOutput, calls=%fused_computation.12 | convolution fusion | flops 21528576 | bytes 1769600 | tf_op jit(solution)/shard_map/lrb,lcb->lrc/dot_general | solution.py:53
  9.1 17.5 %all_to_all.20 = bf16[32,16,144]{2,1,0:T(8,128)(2,1)} all-to-all(bf16[32,16,144]{2,1,0:T(8,128)(2,1)S(1)} %fusion.2), channel_id=1, replica_groups=mesh['sub'=8,'grp'=4] {'sub','grp'}, dimensions={0} | all-to-all | bytes 294912 | tf_op jit(solution)/shard_map/all_to_all | solution.py:8
  26.6 1.3 reshape.70
  27.9 1.7 %convolution_convert_fusion.1 = bf16[32,2304]{1,0:T(8,128)(2,1)} fusion(bf16[32,2304]{1,0:T(8,128)(2,1)S(1)} %reshape.70, s32[32]{0:T(128)} %bitcast.41), kind=kOutput, calls=%fused_computation.2 | convolution fusion | flops 2451968 | bytes 295040 | tf_op jit(solution)/shard_map/of,ok->fk/dot_general | solution.py:44
  29.5 2.0 %reshape.71 = bf16[32,16,144]{2,1,0:T(8,128)(2,1)} reshape(bf16[32,2304]{1,0:T(8,128)(2,1)} %convolution_convert_fusion.1) | data formatting | bytes 294912 | tf_op jit(solution)/shard_map/reshape | solution.py:47
  31.6 12.9 %all_to_all.21 = bf16[32,16,144]{2,1,0:T(8,128)(2,1)S(1)} all-to-all(bf16[32,16,144]{2,1,0:T(8,128)(2,1)} %reshape.71), channel_id=1, replica_groups=mesh['sub'=8,'grp'=4] {'sub','grp'}, dimensions={0} | all-to-all | bytes 294912 | tf_op jit(solution)/shard_map/all_to_all | solution.py:12
  44.5 0.7 copy-done.2
  45.2 1.1 convolution_bitcast_fusion.1
  46.3 1.6 %fusion.9 = f32[512,16]{1,0:T(8,128)} fusion(f32[16,64]{1,0:T(8,128)S(1)} %convolution_bitcast_fusion.1, s32[64]{0:T(128)} %bitcast.43), kind=kOutput, calls=%fused_computation.24 | convolution fusion | flops 6324224 | bytes 37120 | tf_op jit(solution)/shard_map/dot_general | solution.py:65
  47.9 41.1 %psum.7 = f32[512,16]{1,0:T(8,128)} all-reduce(f32[512,16]{1,0:T(8,128)} %fusion.9), channel_id=1, replica_groups=mesh['sub'=8,'grp'=4] {'sub','grp'}, use_global_device_ids=true, to_apply=%region_0.1 | all-reduce | flops 8192 | bytes 65536 | tf_op jit(solution)/shard_map/psum | solution.py:66
  89.0 1.6 %convolution_bitcast_fusion.2 = f32[128,16]{0,1:T(8,128)S(1)} fusion(f32[512,16]{1,0:T(8,128)} %psum.7, f32[128,512]{1,0:T(8,128)} %param.19), kind=kOutput, calls=%fused_computation.15 | convolution fusion | flops 12582912 | bytes 303104 | tf_op jit(solution)/shard_map/dot_general | solution.py:67
  90.7 13.1 %all_gather.3 = f32[512,16]{0,1:T(8,128)S(1)} all-gather(f32[128,16]{0,1:T(8,128)S(1)} %convolution_bitcast_fusion.2), channel_id=1, replica_groups=mesh['sub'=8,'grp'=4] {'grp'}, dimensions={0}, use_global_device_ids=true | all-gather | bytes 40960 | tf_op jit(solution)/shard_map/all_gather | solution.py:68
  104.3 2.4 %fusion.3 = bf16[32,16,144]{2,1,0:T(8,128)(2,1)S(1)} fusion(f32[32,16,144]{2,1,0:T(8,128)S(1)} %convolution_bitcast_fusion, bf16[32,144,144]{2,1,0:T(8,128)(2,1)} %param.16, f32[32]{0:T(128)S(1)} %copy-done.6, bf16[32,16,144]{2,1,0:T(8,128)(2,1)S(1)} %copy-done.3), kind=kOutput, calls=%fused_computation.13 | convolution fusion | flops 21676032 | bytes 1917056 | tf_op jit(solution)/shard_map/lrb,lcb->lrc/dot_general | solution.py:75
  106.7 13.0 %all_to_all.22 = bf16[32,16,144]{2,1,0:T(8,128)(2,1)S(1)} all-to-all(bf16[32,16,144]{2,1,0:T(8,128)(2,1)S(1)} %fusion.3), channel_id=1, replica_groups=mesh['sub'=8,'grp'=4] {'sub','grp'}, dimensions={0} | all-to-all | bytes 294912 | tf_op jit(solution)/shard_map/all_to_all | solution.py:8
  120.3 0.4 reshape.73
  120.7 12.7 %all_to_all.23 = bf16[32,16,144]{2,1,0:T(8,128)(2,1)S(1)} all-to-all(bf16[32,16,144]{2,1,0:T(8,128)(2,1)S(1)} %reshape.73), channel_id=1, replica_groups=mesh['sub'=8,'grp'=4] {'sub','grp'}, dimensions={0} | all-to-all | bytes 294912 | tf_op jit(solution)/shard_map/all_to_all | solution.py:12
  133.4 0.4 fusion.21
  134.5 0.9 fusion.7
  135.4 4.7 %convolution_convert_fusion.4 = bf16[64,16,144]{2,1,0:T(8,128)(2,1)} fusion(bf16[64,144,144]{2,1,0:T(8,128)(2,1)} %param.13, f32[64,16,144]{2,0,1:T(8,128)S(1)} %fusion.7, bf16[64,16,144]{2,1,0:T(8,128)(2,1)} %param.11), kind=kOutput, calls=%fused_computation.5 | convolution fusion | flops 43057152 | bytes 3833856 | tf_op jit(solution)/shard_map/erb,ecb->erc/dot_general | solution.py:90
  140.1 0.7 copy.22
  (24 shorter events, 1.7 us)
Async XLA Ops:
  0.6 6.6 %copy-start = (bf16[32,144,144]{2,1,0:T(8,128)(2,1)S(1)}, bf16[32,144,144]{2,1,0:T(8,128)(2,1)}, u32[]{:S(2)}) copy-start(bf16[32,144,144]{2,1,0:T(8,128)(2,1)} %param.14) | copy-start | bytes 3981316
  1.5 5.8 %copy-start.5 = (f32[32]{0:T(128)}, f32[32]{0:T(128)S(1)}, u32[]{:S(2)}) copy-start(f32[32]{0:T(128)S(1)} %fusion.20) | copy-start | bytes 388
  7.3 38.0 %copy-start.1 = (bf16[32,64,144]{2,1,0:T(8,128)(2,1)S(1)}, bf16[32,64,144]{2,1,0:T(8,128)(2,1)}, u32[]{:S(2)}) copy-start(bf16[32,64,144]{2,1,0:T(8,128)(2,1)} %param.17) | copy-start | bytes 1769476
  29.5 74.3 %copy-start.7 = (s32[1,64]{1,0:T(1,128)S(1)}, s32[1,64]{1,0:T(1,128)}, u32[]{:S(2)}) copy-start(s32[1,64]{1,0:T(1,128)} %param.18) | copy-start | bytes 772
  31.6 72.7 %copy-start.6 = (f32[32]{0:T(128)S(1)}, f32[32]{0:T(128)}, u32[]{:S(2)}) copy-start(f32[32]{0:T(128)} %copy-done.5) | copy-start | bytes 388
  44.5 0.7 copy-start.2
  89.0 15.2 %copy-start.3 = (bf16[32,16,144]{2,1,0:T(8,128)(2,1)S(1)}, bf16[32,16,144]{2,1,0:T(8,128)(2,1)}, u32[]{:S(2)}) copy-start(bf16[32,16,144]{2,1,0:T(8,128)(2,1)} %copy-done.2) | copy-start | bytes 442372
  104.3 15.7 %copy-start.4 = (s32[1,32]{1,0:T(1,128)S(1)}, s32[1,32]{1,0:T(1,128)}, u32[]{:S(2)}) copy-start(s32[1,32]{1,0:T(1,128)} %param.20) | copy-start | bytes 388
  133.4 1.1 copy-start.8
where the time goes:
time: 141 us
  blocking collectives  110 us (78%)
  matrix products  20.8 us (15%)
  local copies, waits for them, and re-layouts  7.45 us (5%)
  other arithmetic  1.48 us (1%)
    psum x1, blocking collectives, body(): coarse_rhs = lax.psum(partial_rhs, ('sub', 'grp'))  41.1 us
    all_to_all x2, blocking collectives, send_out(): lax.all_to_all(partials, ('sub', 'grp'), split_axis=0, concat_axis=0, til...  30.4 us
    all_to_all x2, blocking collectives, send_back(): lax.all_to_all(spread, ('sub', 'grp'), split_axis=0, concat_axis=0, tiled...  25.6 us
    all_gather x1, blocking collectives, body(): coarse_sol = lax.all_gather(row_part, 'grp', axis=0, tiled=True)  13.1 us
    dot_general x1, matrix products, body(): jnp.einsum('erb,ecb->erc', inner_rhs, inner_inv, preferred_element_type=j...  4.68 us
    dot_general x1, matrix products, body(): jnp.einsum('erb,ecb->erc', res_inner, inner_inv, preferred_element_type=j...  3.82 us

commit v1 on v0

--- a/solution.py
+++ b/solution.py
@@ -2,6 +2,7 @@
 import jax.numpy as jnp
 from jax import lax
 from jax.sharding import PartitionSpec as P
+from jax.lax import psum
 
 
 def send_out(partials):
@@ -63,7 +64,7 @@
         coarse_map[0][None, :] == jnp.arange(num_coarse, dtype=jnp.int32)[:, None]
     ).astype(jnp.float32)
     partial_rhs = jnp.dot(coarse_onehot, local_coarse, precision=lax.Precision.HIGHEST)
-    coarse_rhs = lax.psum(partial_rhs, ("sub", "grp"))
+    coarse_rhs = psum(psum(partial_rhs, "grp"), "sub")
     row_part = jnp.dot(coarse_inv, coarse_rhs, precision=lax.Precision.HIGHEST)
     coarse_sol = lax.all_gather(row_part, "grp", axis=0, tiled=True)
     picked = jnp.einsum(

time: 141 us -> 149 us (1.057)
  blocking collectives: 110 us -> 117 us
    psum x1 -> x2, blocking collectives: 41.1 us -> 49.2 us  [body(): coarse_rhs = psum(psum(partial_rhs, 'grp'), 'sub')]
where the time goes in v1:
time: 149 us; the launch traced here: 148 us
  blocking collectives  117 us (79%)
  matrix products  20.9 us (14%)
  local copies, waits for them, and re-layouts  7.45 us (5%)
    psum x2, blocking collectives, body(): coarse_rhs = psum(psum(partial_rhs, 'grp'), 'sub')  49.2 us
    all_to_all x2, blocking collectives, send_out(): lax.all_to_all(partials, ('sub', 'grp'), split_axis=0, concat_axis=0, til...  29.4 us
    all_to_all x2, blocking collectives, send_back(): lax.all_to_all(spread, ('sub', 'grp'), split_axis=0, concat_axis=0, tiled...  25.6 us
    all_gather x1, blocking collectives, body(): coarse_sol = lax.all_gather(row_part, 'grp', axis=0, tiled=True)  13.1 us
    dot_general x1, matrix products, body(): jnp.einsum('erb,ecb->erc', inner_rhs, inner_inv, preferred_element_type=j...  4.68 us
    dot_general x1, matrix products, body(): jnp.einsum('erb,ecb->erc', res_inner, inner_inv, preferred_element_type=j...  3.82 us

profile of v1, /device:TPU:0, one launch (start us, length us, event | category | flops | bytes accessed | tf_op | source)
XLA Modules:
  0.0 147.9 jit_solution(3697326808426598922)
XLA Ops:
  0.6 0.8 fusion.20
  1.5 0.7 fusion.19
  2.1 3.8 %convolution_convert_fusion.5 = bf16[64,16,144]{2,1,0:T(8,128)(2,1)S(1)} fusion(bf16[64,16,144]{2,1,0:T(8,128)(2,1)} %param.11, bf16[64,144,144]{2,1,0:T(8,128)(2,1)} %param.13), kind=kOutput, calls=%fused_computation.6 | convolution fusion | flops 42614784 | bytes 3244032 | tf_op jit(solution)/shard_map/erb,ecb->erc/dot_general | solution.py:50
  6.0 1.3 gather_fusion
  7.3 1.8 %fusion.2 = bf16[32,16,144]{2,1,0:T(8,128)(2,1)S(1)} fusion(bf16[32,16,144]{2,1,0:T(8,128)(2,1)} %gather_fusion, bf16[32,144,144]{2,1,0:T(8,128)(2,1)S(1)} %copy-done, bf16[32,16,144]{2,1,0:T(8,128)(2,1)} %param.12, f32[32]{0:T(128)S(1)} %fusion.20), kind=kOutput, calls=%fused_computation.12 | convolution fusion | flops 21528576 | bytes 1769600 | tf_op jit(solution)/shard_map/lrb,lcb->lrc/dot_general | solution.py:54
  9.1 17.5 %all_to_all.20 = bf16[32,16,144]{2,1,0:T(8,128)(2,1)} all-to-all(bf16[32,16,144]{2,1,0:T(8,128)(2,1)S(1)} %fusion.2), channel_id=1, replica_groups=mesh['sub'=8,'grp'=4] {'sub','grp'}, dimensions={0} | all-to-all | bytes 294912 | tf_op jit(solution)/shard_map/all_to_all | solution.py:9
  26.6 1.3 reshape.70
  27.9 1.7 %convolution_convert_fusion.1 = bf16[32,2304]{1,0:T(8,128)(2,1)} fusion(bf16[32,2304]{1,0:T(8,128)(2,1)S(1)} %reshape.70, s32[32]{0:T(128)} %bitcast.41), kind=kOutput, calls=%fused_computation.2 | convolution fusion | flops 2451968 | bytes 295040 | tf_op jit(solution)/shard_map/of,ok->fk/dot_general | solution.py:45
  29.5 2.0 %reshape.71 = bf16[32,16,144]{2,1,0:T(8,128)(2,1)} reshape(bf16[32,2304]{1,0:T(8,128)(2,1)} %convolution_convert_fusion.1) | data formatting | bytes 294912 | tf_op jit(solution)/shard_map/reshape | solution.py:48
  31.6 12.9 %all_to_all.21 = bf16[32,16,144]{2,1,0:T(8,128)(2,1)S(1)} all-to-all(bf16[32,16,144]{2,1,0:T(8,128)(2,1)} %reshape.71), channel_id=1, replica_groups=mesh['sub'=8,'grp'=4] {'sub','grp'}, dimensions={0} | all-to-all | bytes 294912 | tf_op jit(solution)/shard_map/all_to_all | solution.py:13
  44.5 0.7 copy-done.2
  45.2 1.2 convolution_bitcast_fusion.1
  46.4 1.6 %fusion.9 = f32[512,16]{1,0:T(8,128)} fusion(f32[16,64]{1,0:T(8,128)S(1)} %convolution_bitcast_fusion.1, s32[64]{0:T(128)} %bitcast.43), kind=kOutput, calls=%fused_computation.24 | convolution fusion | flops 6324224 | bytes 37120 | tf_op jit(solution)/shard_map/dot_general | solution.py:66
  48.0 23.1 %psum.14 = f32[512,16]{1,0:T(8,128)} all-reduce(f32[512,16]{1,0:T(8,128)} %fusion.9), channel_id=1, replica_groups=mesh['sub'=8,'grp'=4] {'grp'}, use_global_device_ids=true, to_apply=%region_0.1 | all-reduce | flops 8192 | bytes 65536 | tf_op jit(solution)/shard_map/psum | solution.py:67
  71.1 26.1 %psum.15 = f32[512,16]{1,0:T(8,128)} all-reduce(f32[512,16]{1,0:T(8,128)} %psum.14), channel_id=1, replica_groups=mesh['sub'=8,'grp'=4] {'sub'}, use_global_device_ids=true, to_apply=%region_1.2 | all-reduce | flops 8192 | bytes 65536 | tf_op jit(solution)/shard_map/psum | solution.py:67
  97.2 1.6 %convolution_bitcast_fusion.2 = f32[128,16]{0,1:T(8,128)S(1)} fusion(f32[512,16]{1,0:T(8,128)} %psum.15, f32[128,512]{1,0:T(8,128)} %param.19), kind=kOutput, calls=%fused_computation.15 | convolution fusion | flops 12582912 | bytes 303104 | tf_op jit(solution)/shard_map/dot_general | solution.py:68
  98.8 13.1 %all_gather.3 = f32[512,16]{0,1:T(8,128)S(1)} all-gather(f32[128,16]{0,1:T(8,128)S(1)} %convolution_bitcast_fusion.2), channel_id=1, replica_groups=mesh['sub'=8,'grp'=4] {'grp'}, dimensions={0}, use_global_device_ids=true | all-gather | bytes 40960 | tf_op jit(solution)/shard_map/all_gather | solution.py:69
  112.4 2.4 %fusion.3 = bf16[32,16,144]{2,1,0:T(8,128)(2,1)S(1)} fusion(f32[32,16,144]{2,1,0:T(8,128)S(1)} %convolution_bitcast_fusion, bf16[32,144,144]{2,1,0:T(8,128)(2,1)} %param.16, f32[32]{0:T(128)S(1)} %copy-done.6, bf16[32,16,144]{2,1,0:T(8,128)(2,1)S(1)} %copy-done.3), kind=kOutput, calls=%fused_computation.13 | convolution fusion | flops 21676032 | bytes 1917056 | tf_op jit(solution)/shard_map/lrb,lcb->lrc/dot_general | solution.py:76
  114.9 11.9 %all_to_all.22 = bf16[32,16,144]{2,1,0:T(8,128)(2,1)S(1)} all-to-all(bf16[32,16,144]{2,1,0:T(8,128)(2,1)S(1)} %fusion.3), channel_id=1, replica_groups=mesh['sub'=8,'grp'=4] {'sub','grp'}, dimensions={0} | all-to-all | bytes 294912 | tf_op jit(solution)/shard_map/all_to_all | solution.py:9
  127.4 0.4 reshape.73
  127.8 12.7 %all_to_all.23 = bf16[32,16,144]{2,1,0:T(8,128)(2,1)S(1)} all-to-all(bf16[32,16,144]{2,1,0:T(8,128)(2,1)S(1)} %reshape.73), channel_id=1, replica_groups=mesh['sub'=8,'grp'=4] {'sub','grp'}, dimensions={0} | all-to-all | bytes 294912 | tf_op jit(solution)/shard_map/all_to_all | solution.py:13
  141.6 0.9 fusion.7
  142.5 4.7 %convolution_convert_fusion.4 = bf16[64,16,144]{2,1,0:T(8,128)(2,1)} fusion(bf16[64,144,144]{2,1,0:T(8,128)(2,1)} %param.13, f32[64,16,144]{2,0,1:T(8,128)S(1)} %fusion.7, bf16[64,16,144]{2,1,0:T(8,128)(2,1)} %param.11), kind=kOutput, calls=%fused_computation.5 | convolution fusion | flops 43057152 | bytes 3833856 | tf_op jit(solution)/shard_map/erb,ecb->erc/dot_general | solution.py:91
  147.2 0.7 copy.22
  (25 shorter events, 2.2 us)
Async XLA Ops:
  0.6 6.6 %copy-start = (bf16[32,144,144]{2,1,0:T(8,128)(2,1)S(1)}, bf16[32,144,144]{2,1,0:T(8,128)(2,1)}, u32[]{:S(2)}) copy-start(bf16[32,144,144]{2,1,0:T(8,128)(2,1)} %param.14) | copy-start | bytes 3981316
  1.5 5.8 %copy-start.5 = (f32[32]{0:T(128)}, f32[32]{0:T(128)S(1)}, u32[]{:S(2)}) copy-start(f32[32]{0:T(128)S(1)} %fusion.20) | copy-start | bytes 388
  7.3 37.9 %copy-start.1 = (bf16[32,64,144]{2,1,0:T(8,128)(2,1)S(1)}, bf16[32,64,144]{2,1,0:T(8,128)(2,1)}, u32[]{:S(2)}) copy-start(bf16[32,64,144]{2,1,0:T(8,128)(2,1)} %param.17) | copy-start | bytes 1769476
  29.5 82.4 %copy-start.7 = (s32[1,64]{1,0:T(1,128)S(1)}, s32[1,64]{1,0:T(1,128)}, u32[]{:S(2)}) copy-start(s32[1,64]{1,0:T(1,128)} %param.18) | copy-start | bytes 772
  44.5 0.7 copy-start.2
  45.2 67.2 %copy-start.6 = (f32[32]{0:T(128)S(1)}, f32[32]{0:T(128)}, u32[]{:S(2)}) copy-start(f32[32]{0:T(128)} %copy-done.5) | copy-start | bytes 388
  97.2 15.2 %copy-start.3 = (bf16[32,16,144]{2,1,0:T(8,128)(2,1)S(1)}, bf16[32,16,144]{2,1,0:T(8,128)(2,1)}, u32[]{:S(2)}) copy-start(bf16[32,16,144]{2,1,0:T(8,128)(2,1)} %copy-done.2) | copy-start | bytes 442372
  112.4 14.7 %copy-start.4 = (s32[1,32]{1,0:T(1,128)S(1)}, s32[1,32]{1,0:T(1,128)}, u32[]{:S(2)}) copy-start(s32[1,32]{1,0:T(1,128)} %param.20) | copy-start | bytes 388
  140.5 1.1 copy-start.8
